TPU v7x, 256 devices: a whole 4x4x8 slice. The times are simulated.
256 devices in a mesh: az: 128 (over z, y, x_hi, core), rd: 2 (over x_lo).
Axes of the slice: x: 4 (x_hi: 2, x_lo: 2; x = x_hi * 2 + x_lo), y: 4, z: 8, core: 2. Of those that a mesh axis runs over, the one named last changes fastest.
Arguments:
- echoes: bfloat16 [2, 2048, 32, 2048], P(None, 'az', None, 'rd'), may hold values from -6 to 6
- pulse_taper: float32 [32], replicated, may hold values from 0.1 to 1.9
- beam_weights: float32 [5], replicated, may hold values from 0.3 to 1
- blanking: int32 [2048, 16], P('az'), may hold values 0 or 1
- cfar_sizes: int32 [6], replicated, may hold values from 1 to 23, as said below
Outputs:
- detection: bfloat16 [2048, 32, 2048], P('az', 'rd')
Inputs may be any that keep to these rules, and one draw needn't show every extreme that they name: `cfar_sizes`: the range guard (entry 0) is 1; the Doppler and azimuth guards (entries 2, 4) are 1 or 2; guard plus window is exactly 24 for range (entries 0, 1), 4 for Doppler (2, 3) and 12 for azimuth (4, 5).
All inputs are finite; a program needn't handle non-finite values. No bound on the sum of `blanking` on one device may be relied on, other than what follows from the above.
Results may differ from a plain program's by a relative error of at most 0.012.
Values may be sent and summed in bfloat16 or wider, within the bound.
A program may use at most 64 MiB of HBM per device.

v0:
```python
import math
import jax
import jax.numpy as jnp
from jax import lax
from jax.sharding import PartitionSpec as P

REACH_R = 24
REACH_D = 4
REACH_A = 12
BLANK_CELLS = 128


def with_halo(cells, sides, width, closed):
    for axis, dim in sides:
        count = lax.axis_size(axis)
        ends = count if closed else count - 1
        head = lax.slice_in_dim(cells, 0, width, axis=dim)
        tail = lax.slice_in_dim(cells, cells.shape[dim] - width, cells.shape[dim], axis=dim)
        cells = jnp.concatenate(
            [
                lax.ppermute(tail, axis, [(i, (i + 1) % count) for i in range(ends)]),
                cells,
                lax.ppermute(head, axis, [((i + 1) % count, i) for i in range(ends)]),
            ],
            axis=dim,
        )
    return cells


def bank_matrix(pulse_taper):
    pulses = pulse_taper.shape[0]
    indices = jnp.arange(pulses, dtype=jnp.int32)
    phases = indices[:, None] * indices[None, :] % pulses
    angles = phases.astype(jnp.float32) * (2.0 * math.pi / pulses)
    cosines = jnp.cos(angles) * pulse_taper[None, :]
    sine_terms = jnp.sin(angles) * pulse_taper[None, :]
    real_row = jnp.stack([cosines, sine_terms], axis=1)
    imag_row = jnp.stack([-sine_terms, cosines], axis=1)
    return jnp.stack([real_row, imag_row], axis=0).astype(jnp.bfloat16)


def window_bands(extended, length, reach, guard):
    rows_index = lax.broadcasted_iota(jnp.int32, (extended, length), 0)
    cols_index = lax.broadcasted_iota(jnp.int32, (extended, length), 1)
    before = cols_index + reach - rows_index
    after = rows_index - cols_index - reach
    leading = ((before > guard) & (before <= reach)).astype(jnp.bfloat16)
    lagging = ((after > guard) & (after <= reach)).astype(jnp.bfloat16)
    return (leading, lagging)


def local(echoes, pulse_taper, beam_weights, blanking, cfar_sizes):
    pulses = pulse_taper.shape[0]
    dwells = echoes.shape[1]
    bank = bank_matrix(pulse_taper)
    spectrum = jnp.einsum("ckdp,dapr->cakr", bank, echoes, preferred_element_type=jnp.float32)
    powers = (spectrum[0] * spectrum[0] + spectrum[1] * spectrum[1]) / pulses
    margin = 0
    beside_all = with_halo(powers, (("az", 0),), 2, True)
    span = dwells + 2 * margin
    integrated = beam_weights[0] * beside_all[0:span]
    for offset in range(1, 5):
        integrated = integrated + beam_weights[offset] * beside_all[offset : offset + span]
    log_power = jnp.log(integrated + 0.05).astype(jnp.bfloat16)
    log_power = with_halo(log_power, (("az", 0),), REACH_A, True)
    center = log_power[REACH_A : REACH_A + dwells]
    local_bins = center.shape[1]
    local_cells = center.shape[2]
    guard_range = cfar_sizes[0]
    guard_doppler = cfar_sizes[2]
    window_doppler = cfar_sizes[3].astype(jnp.float32)
    guard_azimuth = cfar_sizes[4]
    window_azimuth = cfar_sizes[5].astype(jnp.float32)
    lead_band, lag_band = window_bands(dwells + 2 * REACH_A, dwells, REACH_A, guard_azimuth)
    azimuth_lead = (
        jnp.einsum("sb,sqr->bqr", lead_band, log_power, preferred_element_type=jnp.float32)
        / window_azimuth
    )
    azimuth_lag = (
        jnp.einsum("sb,sqr->bqr", lag_band, log_power, preferred_element_type=jnp.float32)
        / window_azimuth
    )
    offset_cells = lax.axis_index("rd") * local_cells
    total_cells = local_cells * lax.axis_size("rd")
    widened = with_halo(center, (("rd", 2),), REACH_R, False)
    positions = offset_cells - REACH_R + jnp.arange(local_cells + 2 * REACH_R, dtype=jnp.int32)
    inside = ((positions >= 0) & (positions < total_cells)).astype(jnp.float32)
    block_count = blanking.shape[1]
    block_ids = jnp.clip(positions // BLANK_CELLS, 0, block_count - 1)
    selector = (block_ids[None, :] == jnp.arange(block_count, dtype=jnp.int32)[:, None]).astype(
        jnp.float32
    )
    weight = (
        jnp.dot(blanking.astype(jnp.float32), selector, precision=lax.Precision.HIGHEST)
        * inside[None, :]
    )
    weighted = widened * weight[:, None, :].astype(jnp.bfloat16)
    pieces = local_cells // BLANK_CELLS
    extent = BLANK_CELLS + 2 * REACH_R
    value_blocks = jnp.stack(
        [
            weighted[:, :, number * BLANK_CELLS : number * BLANK_CELLS + extent]
            for number in range(pieces)
        ],
        axis=2,
    )
    weight_blocks = jnp.stack(
        [
            weight[:, number * BLANK_CELLS : number * BLANK_CELLS + extent]
            for number in range(pieces)
        ],
        axis=1,
    )
    range_lead_band, range_lag_band = window_bands(extent, BLANK_CELLS, REACH_R, guard_range)

    def range_mean(banded):
        sums = jnp.einsum("aqbs,sr->aqbr", value_blocks, banded, preferred_element_type=jnp.float32)
        sums = sums.reshape(dwells, local_bins, local_cells)
        counts = jnp.einsum(
            "abs,sr->abr",
            weight_blocks,
            banded.astype(jnp.float32),
            precision=lax.Precision.HIGHEST,
        )
        counts = counts.reshape(dwells, local_cells)
        return sums / jnp.maximum(counts, 1.0)[:, None, :]

    range_lead = range_mean(range_lead_band)
    range_lag = range_mean(range_lag_band)
    circled = jnp.concatenate(
        [center[:, local_bins - REACH_D :], center, center[:, :REACH_D]], axis=1
    )
    doppler_lead_band, doppler_lag_band = window_bands(
        local_bins + 2 * REACH_D, local_bins, REACH_D, guard_doppler
    )
    doppler_lead = (
        jnp.einsum("asr,sk->akr", circled, doppler_lead_band, preferred_element_type=jnp.float32)
        / window_doppler
    )
    doppler_lag = (
        jnp.einsum("asr,sk->akr", circled, doppler_lag_band, preferred_element_type=jnp.float32)
        / window_doppler
    )
    noise_level = jnp.maximum(
        jnp.maximum(range_lead, range_lag), jnp.maximum(doppler_lead, doppler_lag)
    )
    noise_level = jnp.maximum(noise_level, jnp.maximum(azimuth_lead, azimuth_lag))
    keep = weight[:, REACH_R : REACH_R + local_cells]
    detection = (keep[:, None, :] * (center.astype(jnp.float32) - noise_level)).astype(jnp.bfloat16)
    detection = lax.all_to_all(detection, "rd", split_axis=1, concat_axis=2, tiled=True)
    return detection


def solution(mesh):
    in_specs = (P(None, "az", None, "rd"), P(), P(), P("az", None), P())
    out_specs = P("az", "rd", None)
    return jax.shard_map(local, mesh=mesh, in_specs=in_specs, out_specs=out_specs, check_vma=False)
```

profile of v0, /device:TPU:1, one launch (start us, length us, event | category | flops | bytes accessed | tf_op | source)
XLA Modules:
  0.0 95.5 jit_solution(6288917200939661095)
XLA Ops:
  0.0 0.7 fusion.75
  0.8 2.3 %convolution_bitcast_fusion = f32[2,16,32,1024]{3,2,1,0:T(8,128)S(1)} fusion(bf16[2,16,32,1024]{3,2,1,0:T(8,128)(2,1)} %param.5, bf16[1,32,2,32]{3,1,2,0:T(8,128)(2,1)S(1)} %get-tuple-element.14, bf16[1,32,2,32]{3,1,2,0:T(8,128)(2,1)S(1)} %get-tuple-element.13), kind=kOutput, calls=%fused_computation.11 | convolution fusion | flops 134234112 | bytes 6299648 | tf_op jit(solution)/shard_map/ckdp,dapr->cakr/dot_general | solution.py:56
  3.1 0.0 copy-start
  3.1 0.7 broadcast_multiply_fusion
  3.8 3.3 %collective-permute-start.1 = (f32[2,32,1024]{2,1,0:T(8,128)S(1)}, f32[2,32,1024]{2,1,0:T(8,128)S(1)}, u32[]{:S(2)}, u32[]{:S(2)}) collective-permute-start(f32[2,32,1024]{2,1,0:T(8,128)S(1)} %get-tuple-element.6), channel_id=1, source_target_pairs={{2,0},{4,2},{6,4},{8,6},{10,8},{12,10},{14,12},{16,14},{18,16},{20... | collective-permute-start | bytes 786440 | tf_op jit(solution)/shard_map/ppermute | solution.py:23
  7.1 0.0 copy-start.6
  7.1 0.0 copy-start.7
  7.1 0.0 copy-start.8
  7.1 1.0 %collective-permute-start = (f32[2,32,1024]{2,1,0:T(8,128)S(1)}, f32[2,32,1024]{2,1,0:T(8,128)S(1)}, u32[]{:S(2)}, u32[]{:S(2)}) collective-permute-start(f32[2,32,1024]{2,1,0:T(8,128)S(1)} %get-tuple-element.5), channel_id=1, source_target_pairs={{0,2},{2,4},{4,6},{6,8},{8,10},{10,12},{12,14},{14,16},{16,18},{18... | collective-permute-start | bytes 786440 | tf_op jit(solution)/shard_map/ppermute | solution.py:21
  8.1 0.0 copy-done
  8.2 0.5 fusion.129
  8.7 0.0 copy-done.6
  8.7 0.7 fusion.127
  9.3 0.0 copy-done.7
  9.3 0.6 fusion.126
  10.0 0.0 copy-done.8
  10.0 0.2 fusion.128
  10.2 0.9 convolution_maximum_fusion
  11.1 0.9 convolution_maximum_fusion.1
  12.0 0.1 slice.178
  14.0 0.7 copy_bitcast_fusion
  14.6 0.0 collective-permute-done.1
  14.7 2.0 %collective-permute-done = f32[2,32,1024]{2,1,0:T(8,128)S(1)} collective-permute-done((f32[2,32,1024]{2,1,0:T(8,128)S(1)}, f32[2,32,1024]{2,1,0:T(8,128)S(1)}, u32[]{:S(2)}, u32[]{:S(2)}) %collective-permute-start) | collective-permute-done | bytes 262176 | tf_op jit(solution)/shard_map/ppermute | solution.py:21
  16.6 0.0 copy-start.3
  16.6 0.7 copy-done.3
  17.3 5.8 %fusion.11 = bf16[16,32,1024]{2,1,0:T(8,128)(2,1)S(1)} fusion(f32[16,32,1024]{2,1,0:T(8,128)S(1)} %fusion.129, f32[2,32,1024]{2,1,0:T(8,128)S(1)} %collective-permute-done.1, f32[2,32,1024]{2,1,0:T(8,128)} %copy-done.3, f32[]{:T(128)} %bitcast.18, f32[]{:T(128)} %bitcast.16, f32[]{:T(128)} %bitcast.14, f32[]{:T(128)} %bitcast.13, f32[]{:T(128)} %bitcast.1, ...), kind=kLoop, calls=%fused_computation.18 | loop fusion | flops 9437184 | bytes 7864340 | tf_op jit(solution)/shard_map/convert_element_type | solution.py:64
  23.2 1.3 %fusion.125 = (bf16[12,32,1024]{2,1,0:T(8,128)(2,1)}, bf16[12,32,1024]{2,1,0:T(8,128)(2,1)}) fusion(bf16[16,32,1024]{2,1,0:T(8,128)(2,1)S(1)} %fusion.11), kind=kLoop, calls=%fused_computation.187 | loop fusion | bytes 3145728 | tf_op jit(solution)/shard_map/slice | solution.py:18
  24.5 0.1 fusion.124
  24.6 0.1 fusion.123
  24.7 10.6 %collective-permute-start.5 = (bf16[12,32,1024]{2,1,0:T(8,128)(2,1)}, bf16[12,32,1024]{2,1,0:T(8,128)(2,1)}, u32[]{:S(2)}, u32[]{:S(2)}) collective-permute-start(bf16[12,32,1024]{2,1,0:T(8,128)(2,1)} %get-tuple-element.12), channel_id=1, source_target_pairs={{2,0},{4,2},{6,4},{8,6},{10,8},{12,10},{14,12},{16,14},{18,16},{20... | collective-permute-start | bytes 2359304 | tf_op jit(solution)/shard_map/ppermute | solution.py:23
  35.3 0.0 collective-permute-start.4
  35.3 2.2 %collective-permute-start.2 = (bf16[16,32,24]{2,1,0:T(8,128)(2,1)S(1)}, bf16[16,32,24]{2,1,0:T(8,128)(2,1)S(1)}, u32[]{:S(2)}, u32[]{:S(2)}) collective-permute-start(bf16[16,32,24]{2,1,0:T(8,128)(2,1)S(1)} %get-tuple-element.8), channel_id=1, source_target_pairs={{0,1},{2,3},{4,5},{6,7},{8,9},{10,11},{12,13},{14,15},{16,17},{18,... | collective-permute-start | bytes 73736 | tf_op jit(solution)/shard_map/ppermute | solution.py:21
  37.5 1.5 %collective-permute-start.3 = (bf16[16,32,24]{2,1,0:T(8,128)(2,1)S(1)}, bf16[16,32,24]{2,1,0:T(8,128)(2,1)S(1)}, u32[]{:S(2)}, u32[]{:S(2)}) collective-permute-start(bf16[16,32,24]{2,1,0:T(8,128)(2,1)S(1)} %get-tuple-element.7), channel_id=1, source_target_pairs={{1,0},{3,2},{5,4},{7,6},{9,8},{11,10},{13,12},{15,14},{17,16},{19,... | collective-permute-start | bytes 73736 | tf_op jit(solution)/shard_map/ppermute | solution.py:23
  39.0 2.6 %fusion.30 = f32[32,16,1024]{2,0,1:T(8,128)} fusion(bf16[16,4,1024]{2,1,0:T(4,128)(2,1)S(1)} %get-tuple-element.10, bf16[16,32,1024]{2,1,0:T(8,128)(2,1)S(1)} %fusion.11, bf16[16,4,1024]{2,1,0:T(4,128)(2,1)S(1)} %get-tuple-element.9, s32[]{:T(128)} %bitcast.42, s32[32]{0:T(128)S(1)} %iota_add_fusion.2), kind=kOutput, calls=%fused_computation.47 | convolution fusion | flops 45880320 | bytes 3408004 | tf_op jit(solution)/shard_map/asr,sk->akr/dot_general | solution.py:137
  41.6 11.1 %collective-permute-done.2 = bf16[16,32,24]{2,1,0:T(8,128)(2,1)S(1)} collective-permute-done((bf16[16,32,24]{2,1,0:T(8,128)(2,1)S(1)}, bf16[16,32,24]{2,1,0:T(8,128)(2,1)S(1)}, u32[]{:S(2)}, u32[]{:S(2)}) %collective-permute-start.2) | collective-permute-done | bytes 24608 | tf_op jit(solution)/shard_map/ppermute | solution.py:21
  52.7 1.1 %collective-permute-done.3 = bf16[16,32,24]{2,1,0:T(8,128)(2,1)S(1)} collective-permute-done((bf16[16,32,24]{2,1,0:T(8,128)(2,1)S(1)}, bf16[16,32,24]{2,1,0:T(8,128)(2,1)S(1)}, u32[]{:S(2)}, u32[]{:S(2)}) %collective-permute-start.3) | collective-permute-done | bytes 24608 | tf_op jit(solution)/shard_map/ppermute | solution.py:23
  53.9 1.9 %concatenate.20 = bf16[16,32,1072]{2,1,0:T(8,128)(2,1)S(1)} concatenate(bf16[16,32,24]{2,1,0:T(8,128)(2,1)S(1)} %collective-permute-done.2, bf16[16,32,1024]{2,1,0:T(8,128)(2,1)S(1)} %fusion.11, bf16[16,32,24]{2,1,0:T(8,128)(2,1)S(1)} %collective-permute-done.3), dimensions={2} | concatenate | bytes 2195456 | tf_op jit(solution)/shard_map/concatenate | solution.py:19
  55.8 0.1 broadcast_multiply_fusion.1
  56.1 3.3 %fusion.26 = f32[16,32,8,128]{3,2,1,0:T(8,128)} fusion(bf16[16,32,8,176]{3,1,0,2:T(8,128)(2,1)S(1)} %fusion.31, s32[]{:T(128)} %bitcast.27), kind=kOutput, calls=%fused_computation.40 | convolution fusion | flops 184662016 | bytes 3538948 | tf_op jit(solution)/shard_map/aqbs,sr->aqbr/dot_general | solution.py:117
  59.4 2.7 %reshape.196 = f32[16,32,1024]{2,1,0:T(8,128)} reshape(f32[16,32,8,128]{3,2,1,0:T(8,128)} %fusion.26) | data formatting | bytes 4194304 | tf_op jit(solution)/shard_map/reshape | solution.py:118
  62.1 3.3 %fusion.28 = f32[16,32,8,128]{3,2,1,0:T(8,128)} fusion(bf16[16,32,8,176]{3,1,0,2:T(8,128)(2,1)S(1)} %fusion.31, s32[]{:T(128)} %bitcast.27, s32[128]{0:T(128)S(1)} %iota_add_fusion.3), kind=kOutput, calls=%fused_computation.42 | convolution fusion | flops 184639488 | bytes 3539460 | tf_op jit(solution)/shard_map/aqbs,sr->aqbr/dot_general | solution.py:117
  65.4 1.7 %reshape.195 = f32[16,32,1024]{2,1,0:T(8,128)S(1)} reshape(f32[16,32,8,128]{3,2,1,0:T(8,128)} %fusion.28) | data formatting | bytes 4194304 | tf_op jit(solution)/shard_map/reshape | solution.py:118
  67.2 0.0 collective-permute-done.5
  67.2 0.0 collective-permute-done.4
  67.2 1.7 %pad_maximum_fusion = bf16[40,32,1024]{2,1,0:T(8,128)(2,1)S(1)} fusion(bf16[12,32,1024]{2,1,0:T(8,128)(2,1)} %collective-permute-done.5, bf16[16,32,1024]{2,1,0:T(8,128)(2,1)S(1)} %fusion.11, bf16[12,32,1024]{2,1,0:T(8,128)(2,1)} %collective-permute-done.4), kind=kLoop, calls=%fused_computation | loop fusion | flops 2621440 | bytes 5242880 | tf_op jit(solution)/shard_map/concatenate | solution.py:19
  68.8 3.7 %fusion = f32[16,32,1024]{2,0,1:T(8,128)S(1)} fusion(bf16[40,32,1024]{2,1,0:T(8,128)(2,1)S(1)} %pad_maximum_fusion, s32[]{:T(128)} %bitcast.47), kind=kOutput, calls=%fused_computation.5 | convolution fusion | flops 41946240 | bytes 4718596 | tf_op jit(solution)/shard_map/sb,sqr->bqr/dot_general | solution.py:80
  72.6 0.0 copy-start.1
  72.6 0.0 copy-start.2
  72.6 0.0 copy-start.4
  72.6 0.0 copy-start.5
  72.6 3.9 %fusion.2 = f32[16,32,1024]{2,0,1:T(8,128)S(1)} fusion(bf16[40,32,1024]{2,1,0:T(8,128)(2,1)S(1)} %pad_maximum_fusion, s32[]{:T(128)} %bitcast.47, s32[16]{0:T(128)S(1)} %iota_add_fusion.1), kind=kOutput, calls=%fused_computation.7 | convolution fusion | flops 41945600 | bytes 4718660 | tf_op jit(solution)/shard_map/sb,sqr->bqr/dot_general | solution.py:76
  76.5 0.0 copy-done.1
  76.5 0.0 copy-done.2
  76.5 0.0 copy-done.4
  76.5 0.0 copy-done.5
  76.5 4.2 %fusion.22 = bf16[16,32,1024]{2,1,0:T(8,128)(2,1)S(1)} fusion(f32[16,32,1024]{2,0,1:T(8,128)S(1)} %fusion, f32[16,32,1024]{2,0,1:T(8,128)S(1)} %fusion.2, f32[32,16,1024]{2,0,1:T(8,128)S(1)} %copy-done.1, f32[16,32,1024]{2,1,0:T(8,128)S(1)} %copy-done.2, f32[16,32,1024]{2,1,0:T(8,128)S(1)} %reshape.195, bf16[16,32,1024]{2,1,0:T(8,128)(2,1)S(1)} %fusion.11, ...), kind=kOutput, calls=%fused_computation.34 | convolution fusion | flops 53745920 | bytes 13041676 | tf_op jit(solution)/shard_map/asr,sk->akr/dot_general | solution.py:141
  80.8 0.6 copy.25
  81.4 11.4 %all_to_all.18 = bf16[16,32,1024]{2,0,1:T(8,128)(2,1)S(1)} all-to-all(bf16[16,32,1024]{2,0,1:T(8,128)(2,1)S(1)} %copy.25), channel_id=1, replica_groups=mesh['az'=128,'rd'=2] {'rd'}, dimensions={1} | all-to-all | bytes 2097152 | tf_op jit(solution)/shard_map/all_to_all | solution.py:150
  92.8 1.1 %copy.26 = bf16[16,16,2,1024]{3,2,1,0:T(2,128)(2,1)S(1)} copy(bf16[16,16,2,1024]{3,0,1,2:T(8,128)(2,1)S(1)} %bitcast.152) | data formatting | bytes 2097152 | tf_op jit(solution)/shard_map/all_to_all | solution.py:150
  93.9 1.6 %all_to_all.16 = bf16[16,16,2048]{2,1,0:T(8,128)(2,1)} reshape(bf16[16,16,2,1024]{3,2,1,0:T(2,128)(2,1)S(1)} %copy.26) | data formatting | bytes 2097152 | tf_op jit(solution)/shard_map/all_to_all | solution.py:150
  (23 shorter events, 0.3 us)
Async XLA Ops:
  3.1 5.0 %copy-start = (f32[2,16,32,1024]{3,2,1,0:T(8,128)}, f32[2,16,32,1024]{3,2,1,0:T(8,128)S(1)}, u32[]{:S(2)}) copy-start(f32[2,16,32,1024]{3,2,1,0:T(8,128)S(1)} %convolution_bitcast_fusion) | copy-start | bytes 12582916
  3.8 10.8 %collective-permute-start.1 = (f32[2,32,1024]{2,1,0:T(8,128)S(1)}, f32[2,32,1024]{2,1,0:T(8,128)S(1)}, u32[]{:S(2)}, u32[]{:S(2)}) collective-permute-start(f32[2,32,1024]{2,1,0:T(8,128)S(1)} %get-tuple-element.6), channel_id=1, source_target_pairs={{2,0},{4,2},{6,4},{8,6},{10,8},{12,10},{14,12},{16,14},{18,16},{20... | collective-permute-start | bytes 786440 | tf_op jit(solution)/shard_map/ppermute | solution.py:23
  7.1 1.6 %copy-start.6 = (f32[5]{0:T(128)S(1)}, f32[5]{0:T(128)}, u32[]{:S(2)}) copy-start(f32[5]{0:T(128)} %param.7) | copy-start | bytes 64
  7.1 2.2 %copy-start.7 = (s32[6]{0:T(128)S(1)}, s32[6]{0:T(128)}, u32[]{:S(2)}) copy-start(s32[6]{0:T(128)} %param.9) | copy-start | bytes 76
  7.1 2.8 %copy-start.8 = (s32[16,16]{1,0:T(8,128)S(1)}, s32[16,16]{1,0:T(8,128)}, u32[]{:S(2)}) copy-start(s32[16,16]{1,0:T(8,128)} %param.8) | copy-start | bytes 3076
  7.1 9.5 %collective-permute-start = (f32[2,32,1024]{2,1,0:T(8,128)S(1)}, f32[2,32,1024]{2,1,0:T(8,128)S(1)}, u32[]{:S(2)}, u32[]{:S(2)}) collective-permute-start(f32[2,32,1024]{2,1,0:T(8,128)S(1)} %get-tuple-element.5), channel_id=1, source_target_pairs={{0,2},{2,4},{4,6},{6,8},{8,10},{10,12},{12,14},{14,16},{16,18},{18... | collective-permute-start | bytes 786440 | tf_op jit(solution)/shard_map/ppermute | solution.py:21
  16.6 0.7 copy-start.3
  24.7 42.4 %collective-permute-start.5 = (bf16[12,32,1024]{2,1,0:T(8,128)(2,1)}, bf16[12,32,1024]{2,1,0:T(8,128)(2,1)}, u32[]{:S(2)}, u32[]{:S(2)}) collective-permute-start(bf16[12,32,1024]{2,1,0:T(8,128)(2,1)} %get-tuple-element.12), channel_id=1, source_target_pairs={{2,0},{4,2},{6,4},{8,6},{10,8},{12,10},{14,12},{16,14},{18,16},{20... | collective-permute-start | bytes 2359304 | tf_op jit(solution)/shard_map/ppermute | solution.py:23
  35.3 31.9 %collective-permute-start.4 = (bf16[12,32,1024]{2,1,0:T(8,128)(2,1)}, bf16[12,32,1024]{2,1,0:T(8,128)(2,1)}, u32[]{:S(2)}, u32[]{:S(2)}) collective-permute-start(bf16[12,32,1024]{2,1,0:T(8,128)(2,1)} %get-tuple-element.11), channel_id=1, source_target_pairs={{0,2},{2,4},{4,6},{6,8},{8,10},{10,12},{12,14},{14,16},{16,18},{18... | collective-permute-start | bytes 2359304 | tf_op jit(solution)/shard_map/ppermute | solution.py:21
  35.3 17.4 %collective-permute-start.2 = (bf16[16,32,24]{2,1,0:T(8,128)(2,1)S(1)}, bf16[16,32,24]{2,1,0:T(8,128)(2,1)S(1)}, u32[]{:S(2)}, u32[]{:S(2)}) collective-permute-start(bf16[16,32,24]{2,1,0:T(8,128)(2,1)S(1)} %get-tuple-element.8), channel_id=1, source_target_pairs={{0,1},{2,3},{4,5},{6,7},{8,9},{10,11},{12,13},{14,15},{16,17},{18,... | collective-permute-start | bytes 73736 | tf_op jit(solution)/shard_map/ppermute | solution.py:21
  37.5 16.3 %collective-permute-start.3 = (bf16[16,32,24]{2,1,0:T(8,128)(2,1)S(1)}, bf16[16,32,24]{2,1,0:T(8,128)(2,1)S(1)}, u32[]{:S(2)}, u32[]{:S(2)}) collective-permute-start(bf16[16,32,24]{2,1,0:T(8,128)(2,1)S(1)} %get-tuple-element.7), channel_id=1, source_target_pairs={{1,0},{3,2},{5,4},{7,6},{9,8},{11,10},{13,12},{15,14},{17,16},{19,... | collective-permute-start | bytes 73736 | tf_op jit(solution)/shard_map/ppermute | solution.py:23
  72.6 3.9 %copy-start.1 = (f32[32,16,1024]{2,0,1:T(8,128)S(1)}, f32[32,16,1024]{2,0,1:T(8,128)}, u32[]{:S(2)}) copy-start(f32[32,16,1024]{2,0,1:T(8,128)} %fusion.30) | copy-start | bytes 6291460
  72.6 3.9 %copy-start.2 = (f32[16,32,1024]{2,1,0:T(8,128)S(1)}, f32[16,32,1024]{2,1,0:T(8,128)}, u32[]{:S(2)}) copy-start(f32[16,32,1024]{2,1,0:T(8,128)} %reshape.196) | copy-start | bytes 6291460
  72.6 3.9 %copy-start.4 = (f32[16,1024]{1,0:T(8,128)S(1)}, f32[16,1024]{1,0:T(8,128)}, u32[]{:S(2)}) copy-start(f32[16,1024]{1,0:T(8,128)} %get-tuple-element.30) | copy-start | bytes 196612
  72.6 3.9 %copy-start.5 = (f32[16,1024]{1,0:T(8,128)S(1)}, f32[16,1024]{1,0:T(8,128)}, u32[]{:S(2)}) copy-start(f32[16,1024]{1,0:T(8,128)} %get-tuple-element.31) | copy-start | bytes 196612
where the time goes:
time: 95.9 us; the launch traced here: 95.5 us
  matrix products  25.4 us (26%)
  starting transfers between devices  18.6 us (19%)
  waiting for transfers between devices  14.2 us (15%)
  local copies, waits for them, and re-layouts  14.1 us (15%)
  blocking collectives  11.4 us (12%)
  other arithmetic  9.52 us (10%)
  between operations  2.24 us (2%)
    ppermute x3, starting transfers between devices, with_halo(): lax.ppermute(head, axis, [((i + 1) % count, i) for i in range(ends)])  15.3 us
    ppermute x3, waiting for transfers between devices, with_halo(): lax.ppermute(tail, axis, [(i, (i + 1) % count) for i in range(ends)])  13.1 us
    all_to_all x1, blocking collectives, local(): lax.all_to_all(detection, 'rd', split_axis=1, concat_axis=2, tiled=True)  11.4 us
    dot_general x2, matrix products, range_mean(): jnp.einsum('aqbs,sr->aqbr', value_blocks, banded, preferred_element_type=...  6.59 us
    convert_element_type x1, other arithmetic, local(): log_power = jnp.log(integrated + 0.05).astype(jnp.bfloat16)  5.83 us
    reshape x2, local copies, waits for them, and re-layouts, range_mean(): sums = sums.reshape(dwells, local_bins, local_cells)  4.41 us
    dot_general x1, matrix products, local(): jnp.einsum('asr,sk->akr', circled, doppler_lag_band, preferred_element_ty...  4.25 us
    dot_general x1, matrix products, local(): jnp.einsum('sb,sqr->bqr', lead_band, log_power, preferred_element_type=jn...  3.89 us
  transfers between devices with their start and end apart: 6, of which 3 were waited for; matrix products, arithmetic and copies ran while one was open for 21% of the time, Pallas kernels for 0%

commit v1 on v0

--- a/solution.py
+++ b/solution.py
@@ -147,7 +147,9 @@
     noise_level = jnp.maximum(noise_level, jnp.maximum(azimuth_lead, azimuth_lag))
     keep = weight[:, REACH_R : REACH_R + local_cells]
     detection = (keep[:, None, :] * (center.astype(jnp.float32) - noise_level)).astype(jnp.bfloat16)
-    detection = lax.all_to_all(detection, "rd", split_axis=1, concat_axis=2, tiled=True)
+    parts = jnp.split(detection, lax.axis_size("rd"), axis=1)
+    got = lax.all_to_all(jnp.stack(parts), "rd", 0, 0)
+    detection = jnp.concatenate(got, axis=2)
     return detection
 
 

time: 95.9 us -> 94.2 us (0.982)
  local copies, waits for them, and re-layouts: 14.1 us -> 12 us
    all_to_all x2 -> x0, local copies, waits for them, and re-layouts: 2.68 us -> none  [local(): lax.all_to_all(detection, 'rd', split_axis=1, concat_axis=2, tiled=True)]
    reshape x0 -> x1, local copies, waits for them, and re-layouts: none -> 1.06 us  [local(): detection = jnp.concatenate(got, axis=2)]
  transfers between devices with their start and end apart: 6 -> 6, of which waited for: 3 -> 3; matrix products, arithmetic and copies ran while one was open for 21% -> 22% of each run, Pallas kernels for 0% -> 0%
where the time goes in v1:
time: 94.2 us; the launch traced here: 93.8 us
  matrix products  25.7 us (27%)
  starting transfers between devices  18.6 us (20%)
  waiting for transfers between devices  14.1 us (15%)
  local copies, waits for them, and re-layouts  12 us (13%)
  blocking collectives  11.4 us (12%)
  other arithmetic  9.58 us (10%)
  between operations  2.29 us (2%)
    ppermute x3, starting transfers between devices, with_halo(): lax.ppermute(head, axis, [((i + 1) % count, i) for i in range(ends)])  15.3 us
    ppermute x3, waiting for transfers between devices, with_halo(): lax.ppermute(tail, axis, [(i, (i + 1) % count) for i in range(ends)])  13 us
    all_to_all x1, blocking collectives, local(): got = lax.all_to_all(jnp.stack(parts), 'rd', 0, 0)  11.4 us
    dot_general x2, matrix products, range_mean(): jnp.einsum('aqbs,sr->aqbr', value_blocks, banded, preferred_element_type=...  6.73 us
    convert_element_type x1, other arithmetic, local(): log_power = jnp.log(integrated + 0.05).astype(jnp.bfloat16)  5.79 us
    reshape x2, local copies, waits for them, and re-layouts, range_mean(): sums = sums.reshape(dwells, local_bins, local_cells)  4.4 us
    dot_general x1, matrix products, local(): jnp.einsum('asr,sk->akr', circled, doppler_lag_band, preferred_element_ty...  4.11 us
    dot_general x1, matrix products, local(): jnp.einsum('sb,sqr->bqr', lead_band, log_power, preferred_element_type=jn...  3.95 us
  transfers between devices with their start and end apart: 6, of which 3 were waited for; matrix products, arithmetic and copies ran while one was open for 22% of the time, Pallas kernels for 0%

profile of v1, /device:TPU:1, one launch (start us, length us, event | category | flops | bytes accessed | tf_op | source)
XLA Modules:
  0.0 93.8 jit_solution(8864147334610873267)
XLA Ops:
  0.0 0.7 fusion.75
  0.8 2.3 %convolution_bitcast_fusion = f32[2,16,32,1024]{3,2,1,0:T(8,128)S(1)} fusion(bf16[2,16,32,1024]{3,2,1,0:T(8,128)(2,1)} %param.5, bf16[1,32,2,32]{3,1,2,0:T(8,128)(2,1)S(1)} %get-tuple-element.16, bf16[1,32,2,32]{3,1,2,0:T(8,128)(2,1)S(1)} %get-tuple-element.15), kind=kOutput, calls=%fused_computation.11 | convolution fusion | flops 134234112 | bytes 6299648 | tf_op jit(solution)/shard_map/ckdp,dapr->cakr/dot_general | solution.py:56
  3.1 0.0 copy-start
  3.1 0.7 broadcast_multiply_fusion
  3.8 3.3 %collective-permute-start.1 = (f32[2,32,1024]{2,1,0:T(8,128)S(1)}, f32[2,32,1024]{2,1,0:T(8,128)S(1)}, u32[]{:S(2)}, u32[]{:S(2)}) collective-permute-start(f32[2,32,1024]{2,1,0:T(8,128)S(1)} %get-tuple-element.6), channel_id=1, source_target_pairs={{2,0},{4,2},{6,4},{8,6},{10,8},{12,10},{14,12},{16,14},{18,16},{20... | collective-permute-start | bytes 786440 | tf_op jit(solution)/shard_map/ppermute | solution.py:23
  7.1 0.0 copy-start.6
  7.1 0.0 copy-start.7
  7.1 0.0 copy-start.8
  7.1 1.0 %collective-permute-start = (f32[2,32,1024]{2,1,0:T(8,128)S(1)}, f32[2,32,1024]{2,1,0:T(8,128)S(1)}, u32[]{:S(2)}, u32[]{:S(2)}) collective-permute-start(f32[2,32,1024]{2,1,0:T(8,128)S(1)} %get-tuple-element.5), channel_id=1, source_target_pairs={{0,2},{2,4},{4,6},{6,8},{8,10},{10,12},{12,14},{14,16},{16,18},{18... | collective-permute-start | bytes 786440 | tf_op jit(solution)/shard_map/ppermute | solution.py:21
  8.1 0.0 copy-done
  8.2 0.5 fusion.129
  8.7 0.0 copy-done.6
  8.7 0.7 fusion.127
  9.3 0.0 copy-done.7
  9.3 0.7 fusion.126
  10.0 0.0 copy-done.8
  10.0 0.2 fusion.128
  10.3 1.0 %convolution_maximum_fusion = f32[16,8,128]{2,1,0:T(8,128)S(1)} fusion(f32[16,8,176]{2,0,1:T(8,128)S(1)} %constant_dynamic-update-slice_fusion, s32[]{:T(128)} %bitcast.27), kind=kOutput, calls=%fused_computation.45 | convolution fusion | flops 34732032 | bytes 155652 | tf_op jit(solution)/shard_map/abs,sr->abr/dot_general | solution.py:119
  11.2 1.0 %convolution_maximum_fusion.1 = f32[16,8,128]{2,1,0:T(8,128)S(1)} fusion(f32[16,8,176]{2,0,1:T(8,128)S(1)} %constant_dynamic-update-slice_fusion, s32[]{:T(128)} %bitcast.27, s32[128]{0:T(128)S(1)} %iota_add_fusion.3), kind=kOutput, calls=%fused_computation.46 | convolution fusion | flops 34709504 | bytes 156164 | tf_op jit(solution)/shard_map/abs,sr->abr/dot_general | solution.py:119
  12.2 0.1 slice.178
  14.2 0.7 copy_bitcast_fusion
  14.9 0.0 collective-permute-done.1
  14.9 1.8 %collective-permute-done = f32[2,32,1024]{2,1,0:T(8,128)S(1)} collective-permute-done((f32[2,32,1024]{2,1,0:T(8,128)S(1)}, f32[2,32,1024]{2,1,0:T(8,128)S(1)}, u32[]{:S(2)}, u32[]{:S(2)}) %collective-permute-start) | collective-permute-done | bytes 262176 | tf_op jit(solution)/shard_map/ppermute | solution.py:21
  16.6 0.0 copy-start.3
  16.6 0.7 copy-done.3
  17.3 5.8 %fusion.11 = bf16[16,32,1024]{2,1,0:T(8,128)(2,1)S(1)} fusion(f32[16,32,1024]{2,1,0:T(8,128)S(1)} %fusion.129, f32[2,32,1024]{2,1,0:T(8,128)S(1)} %collective-permute-done.1, f32[2,32,1024]{2,1,0:T(8,128)} %copy-done.3, f32[]{:T(128)} %bitcast.18, f32[]{:T(128)} %bitcast.16, f32[]{:T(128)} %bitcast.14, f32[]{:T(128)} %bitcast.13, f32[]{:T(128)} %bitcast.1, ...), kind=kLoop, calls=%fused_computation.18 | loop fusion | flops 9437184 | bytes 7864340 | tf_op jit(solution)/shard_map/convert_element_type | solution.py:64
  23.1 1.3 %fusion.125 = (bf16[12,32,1024]{2,1,0:T(8,128)(2,1)}, bf16[12,32,1024]{2,1,0:T(8,128)(2,1)}) fusion(bf16[16,32,1024]{2,1,0:T(8,128)(2,1)S(1)} %fusion.11), kind=kLoop, calls=%fused_computation.190 | loop fusion | bytes 3145728 | tf_op jit(solution)/shard_map/slice | solution.py:18
  24.5 0.1 fusion.124
  24.6 0.1 fusion.123
  24.7 10.6 %collective-permute-start.5 = (bf16[12,32,1024]{2,1,0:T(8,128)(2,1)}, bf16[12,32,1024]{2,1,0:T(8,128)(2,1)}, u32[]{:S(2)}, u32[]{:S(2)}) collective-permute-start(bf16[12,32,1024]{2,1,0:T(8,128)(2,1)} %get-tuple-element.14), channel_id=1, source_target_pairs={{2,0},{4,2},{6,4},{8,6},{10,8},{12,10},{14,12},{16,14},{18,16},{20... | collective-permute-start | bytes 2359304 | tf_op jit(solution)/shard_map/ppermute | solution.py:23
  35.3 0.0 collective-permute-start.4
  35.3 2.2 %collective-permute-start.2 = (bf16[16,32,24]{2,1,0:T(8,128)(2,1)S(1)}, bf16[16,32,24]{2,1,0:T(8,128)(2,1)S(1)}, u32[]{:S(2)}, u32[]{:S(2)}) collective-permute-start(bf16[16,32,24]{2,1,0:T(8,128)(2,1)S(1)} %get-tuple-element.10), channel_id=1, source_target_pairs={{0,1},{2,3},{4,5},{6,7},{8,9},{10,11},{12,13},{14,15},{16,17},{18,... | collective-permute-start | bytes 73736 | tf_op jit(solution)/shard_map/ppermute | solution.py:21
  37.5 1.5 %collective-permute-start.3 = (bf16[16,32,24]{2,1,0:T(8,128)(2,1)S(1)}, bf16[16,32,24]{2,1,0:T(8,128)(2,1)S(1)}, u32[]{:S(2)}, u32[]{:S(2)}) collective-permute-start(bf16[16,32,24]{2,1,0:T(8,128)(2,1)S(1)} %get-tuple-element.9), channel_id=1, source_target_pairs={{1,0},{3,2},{5,4},{7,6},{9,8},{11,10},{13,12},{15,14},{17,16},{19,... | collective-permute-start | bytes 73736 | tf_op jit(solution)/shard_map/ppermute | solution.py:23
  39.0 2.7 %fusion.30 = f32[32,16,1024]{2,0,1:T(8,128)} fusion(bf16[16,4,1024]{2,1,0:T(4,128)(2,1)S(1)} %get-tuple-element.12, bf16[16,32,1024]{2,1,0:T(8,128)(2,1)S(1)} %fusion.11, bf16[16,4,1024]{2,1,0:T(4,128)(2,1)S(1)} %get-tuple-element.11, s32[]{:T(128)} %bitcast.42, s32[32]{0:T(128)S(1)} %iota_add_fusion.2), kind=kOutput, calls=%fused_computation.47 | convolution fusion | flops 45880320 | bytes 3408004 | tf_op jit(solution)/shard_map/asr,sk->akr/dot_general | solution.py:137
  41.7 11.2 %collective-permute-done.2 = bf16[16,32,24]{2,1,0:T(8,128)(2,1)S(1)} collective-permute-done((bf16[16,32,24]{2,1,0:T(8,128)(2,1)S(1)}, bf16[16,32,24]{2,1,0:T(8,128)(2,1)S(1)}, u32[]{:S(2)}, u32[]{:S(2)}) %collective-permute-start.2) | collective-permute-done | bytes 24608 | tf_op jit(solution)/shard_map/ppermute | solution.py:21
  52.9 1.1 %collective-permute-done.3 = bf16[16,32,24]{2,1,0:T(8,128)(2,1)S(1)} collective-permute-done((bf16[16,32,24]{2,1,0:T(8,128)(2,1)S(1)}, bf16[16,32,24]{2,1,0:T(8,128)(2,1)S(1)}, u32[]{:S(2)}, u32[]{:S(2)}) %collective-permute-start.3) | collective-permute-done | bytes 24608 | tf_op jit(solution)/shard_map/ppermute | solution.py:23
  54.0 1.9 %concatenate.20 = bf16[16,32,1072]{2,1,0:T(8,128)(2,1)S(1)} concatenate(bf16[16,32,24]{2,1,0:T(8,128)(2,1)S(1)} %collective-permute-done.2, bf16[16,32,1024]{2,1,0:T(8,128)(2,1)S(1)} %fusion.11, bf16[16,32,24]{2,1,0:T(8,128)(2,1)S(1)} %collective-permute-done.3), dimensions={2} | concatenate | bytes 2195456 | tf_op jit(solution)/shard_map/concatenate | solution.py:19
  56.0 0.1 broadcast_multiply_fusion.1
  56.3 3.4 %fusion.26 = f32[16,32,8,128]{3,2,1,0:T(8,128)} fusion(bf16[16,32,8,176]{3,1,0,2:T(8,128)(2,1)S(1)} %fusion.31, s32[]{:T(128)} %bitcast.27), kind=kOutput, calls=%fused_computation.40 | convolution fusion | flops 184662016 | bytes 3538948 | tf_op jit(solution)/shard_map/aqbs,sr->aqbr/dot_general | solution.py:117
  59.7 2.7 %reshape.202 = f32[16,32,1024]{2,1,0:T(8,128)} reshape(f32[16,32,8,128]{3,2,1,0:T(8,128)} %fusion.26) | data formatting | bytes 4194304 | tf_op jit(solution)/shard_map/reshape | solution.py:118
  62.4 3.4 %fusion.28 = f32[16,32,8,128]{3,2,1,0:T(8,128)} fusion(bf16[16,32,8,176]{3,1,0,2:T(8,128)(2,1)S(1)} %fusion.31, s32[]{:T(128)} %bitcast.27, s32[128]{0:T(128)S(1)} %iota_add_fusion.3), kind=kOutput, calls=%fused_computation.42 | convolution fusion | flops 184639488 | bytes 3539460 | tf_op jit(solution)/shard_map/aqbs,sr->aqbr/dot_general | solution.py:117
  65.8 1.7 %reshape.201 = f32[16,32,1024]{2,1,0:T(8,128)S(1)} reshape(f32[16,32,8,128]{3,2,1,0:T(8,128)} %fusion.28) | data formatting | bytes 4194304 | tf_op jit(solution)/shard_map/reshape | solution.py:118
  67.5 0.0 collective-permute-done.5
  67.5 0.0 collective-permute-done.4
  67.5 1.7 %pad_maximum_fusion = bf16[40,32,1024]{2,1,0:T(8,128)(2,1)S(1)} fusion(bf16[12,32,1024]{2,1,0:T(8,128)(2,1)} %collective-permute-done.5, bf16[16,32,1024]{2,1,0:T(8,128)(2,1)S(1)} %fusion.11, bf16[12,32,1024]{2,1,0:T(8,128)(2,1)} %collective-permute-done.4), kind=kLoop, calls=%fused_computation | loop fusion | flops 2621440 | bytes 5242880 | tf_op jit(solution)/shard_map/concatenate | solution.py:19
  69.2 3.8 %fusion = f32[16,32,1024]{2,0,1:T(8,128)S(1)} fusion(bf16[40,32,1024]{2,1,0:T(8,128)(2,1)S(1)} %pad_maximum_fusion, s32[]{:T(128)} %bitcast.47), kind=kOutput, calls=%fused_computation.5 | convolution fusion | flops 41946240 | bytes 4718596 | tf_op jit(solution)/shard_map/sb,sqr->bqr/dot_general | solution.py:80
  73.0 0.0 copy-start.1
  73.0 0.0 copy-start.2
  73.0 0.0 copy-start.4
  73.0 0.0 copy-start.5
  73.0 3.9 %fusion.2 = f32[16,32,1024]{2,0,1:T(8,128)S(1)} fusion(bf16[40,32,1024]{2,1,0:T(8,128)(2,1)S(1)} %pad_maximum_fusion, s32[]{:T(128)} %bitcast.47, s32[16]{0:T(128)S(1)} %iota_add_fusion.1), kind=kOutput, calls=%fused_computation.7 | convolution fusion | flops 41945600 | bytes 4718660 | tf_op jit(solution)/shard_map/sb,sqr->bqr/dot_general | solution.py:76
  76.9 0.0 copy-done.1
  76.9 0.0 copy-done.2
  76.9 0.0 copy-done.4
  76.9 0.0 copy-done.5
  77.0 4.1 %fusion.22 = bf16[16,32,1024]{2,1,0:T(8,128)(2,1)S(1)} fusion(f32[16,32,1024]{2,0,1:T(8,128)S(1)} %fusion, f32[16,32,1024]{2,0,1:T(8,128)S(1)} %fusion.2, f32[32,16,1024]{2,0,1:T(8,128)S(1)} %copy-done.1, f32[16,32,1024]{2,1,0:T(8,128)S(1)} %copy-done.2, f32[16,32,1024]{2,1,0:T(8,128)S(1)} %reshape.201, bf16[16,32,1024]{2,1,0:T(8,128)(2,1)S(1)} %fusion.11, ...), kind=kOutput, calls=%fused_computation.34 | convolution fusion | flops 53745920 | bytes 13041676 | tf_op jit(solution)/shard_map/asr,sk->akr/dot_general | solution.py:141
  81.1 0.1 slice_bitcast_fusion.1
  81.2 0.1 pad_maximum_fusion.6
  81.3 11.4 %all_to_all.5 = bf16[2,16,16,1024]{3,2,1,0:T(8,128)(2,1)S(1)} all-to-all(bf16[2,16,16,1024]{3,2,1,0:T(8,128)(2,1)S(1)} %pad_maximum_fusion.6), channel_id=1, replica_groups=mesh['az'=128,'rd'=2] {'rd'}, dimensions={0} | all-to-all | bytes 2097152 | tf_op jit(solution)/shard_map/all_to_all | solution.py:151
  92.7 1.1 %copy.29 = bf16[2,16,2,8,1024]{4,3,0,2,1:T(8,128)(2,1)} copy(bf16[2,16,2,8,1024]{4,3,2,1,0:T(8,128)(2,1)S(1)} %bitcast.156) | data formatting | bytes 2097152 | tf_op jit(solution)/shard_map/reshape | solution.py:152
  (23 shorter events, 0.3 us)
Async XLA Ops:
  3.1 5.0 %copy-start = (f32[2,16,32,1024]{3,2,1,0:T(8,128)}, f32[2,16,32,1024]{3,2,1,0:T(8,128)S(1)}, u32[]{:S(2)}) copy-start(f32[2,16,32,1024]{3,2,1,0:T(8,128)S(1)} %convolution_bitcast_fusion) | copy-start | bytes 12582916
  3.8 11.0 %collective-permute-start.1 = (f32[2,32,1024]{2,1,0:T(8,128)S(1)}, f32[2,32,1024]{2,1,0:T(8,128)S(1)}, u32[]{:S(2)}, u32[]{:S(2)}) collective-permute-start(f32[2,32,1024]{2,1,0:T(8,128)S(1)} %get-tuple-element.6), channel_id=1, source_target_pairs={{2,0},{4,2},{6,4},{8,6},{10,8},{12,10},{14,12},{16,14},{18,16},{20... | collective-permute-start | bytes 786440 | tf_op jit(solution)/shard_map/ppermute | solution.py:23
  7.1 1.6 %copy-start.6 = (f32[5]{0:T(128)S(1)}, f32[5]{0:T(128)}, u32[]{:S(2)}) copy-start(f32[5]{0:T(128)} %param.7) | copy-start | bytes 64
  7.1 2.2 %copy-start.7 = (s32[6]{0:T(128)S(1)}, s32[6]{0:T(128)}, u32[]{:S(2)}) copy-start(s32[6]{0:T(128)} %param.9) | copy-start | bytes 76
  7.1 2.9 %copy-start.8 = (s32[16,16]{1,0:T(8,128)S(1)}, s32[16,16]{1,0:T(8,128)}, u32[]{:S(2)}) copy-start(s32[16,16]{1,0:T(8,128)} %param.8) | copy-start | bytes 3076
  7.1 9.5 %collective-permute-start = (f32[2,32,1024]{2,1,0:T(8,128)S(1)}, f32[2,32,1024]{2,1,0:T(8,128)S(1)}, u32[]{:S(2)}, u32[]{:S(2)}) collective-permute-start(f32[2,32,1024]{2,1,0:T(8,128)S(1)} %get-tuple-element.5), channel_id=1, source_target_pairs={{0,2},{2,4},{4,6},{6,8},{8,10},{10,12},{12,14},{14,16},{16,18},{18... | collective-permute-start | bytes 786440 | tf_op jit(solution)/shard_map/ppermute | solution.py:21
  16.6 0.7 copy-start.3
  24.7 42.8 %collective-permute-start.5 = (bf16[12,32,1024]{2,1,0:T(8,128)(2,1)}, bf16[12,32,1024]{2,1,0:T(8,128)(2,1)}, u32[]{:S(2)}, u32[]{:S(2)}) collective-permute-start(bf16[12,32,1024]{2,1,0:T(8,128)(2,1)} %get-tuple-element.14), channel_id=1, source_target_pairs={{2,0},{4,2},{6,4},{8,6},{10,8},{12,10},{14,12},{16,14},{18,16},{20... | collective-permute-start | bytes 2359304 | tf_op jit(solution)/shard_map/ppermute | solution.py:23
  35.3 32.2 %collective-permute-start.4 = (bf16[12,32,1024]{2,1,0:T(8,128)(2,1)}, bf16[12,32,1024]{2,1,0:T(8,128)(2,1)}, u32[]{:S(2)}, u32[]{:S(2)}) collective-permute-start(bf16[12,32,1024]{2,1,0:T(8,128)(2,1)} %get-tuple-element.13), channel_id=1, source_target_pairs={{0,2},{2,4},{4,6},{6,8},{8,10},{10,12},{12,14},{14,16},{16,18},{18... | collective-permute-start | bytes 2359304 | tf_op jit(solution)/shard_map/ppermute | solution.py:21
  35.3 17.6 %collective-permute-start.2 = (bf16[16,32,24]{2,1,0:T(8,128)(2,1)S(1)}, bf16[16,32,24]{2,1,0:T(8,128)(2,1)S(1)}, u32[]{:S(2)}, u32[]{:S(2)}) collective-permute-start(bf16[16,32,24]{2,1,0:T(8,128)(2,1)S(1)} %get-tuple-element.10), channel_id=1, source_target_pairs={{0,1},{2,3},{4,5},{6,7},{8,9},{10,11},{12,13},{14,15},{16,17},{18,... | collective-permute-start | bytes 73736 | tf_op jit(solution)/shard_map/ppermute | solution.py:21
  37.5 16.5 %collective-permute-start.3 = (bf16[16,32,24]{2,1,0:T(8,128)(2,1)S(1)}, bf16[16,32,24]{2,1,0:T(8,128)(2,1)S(1)}, u32[]{:S(2)}, u32[]{:S(2)}) collective-permute-start(bf16[16,32,24]{2,1,0:T(8,128)(2,1)S(1)} %get-tuple-element.9), channel_id=1, source_target_pairs={{1,0},{3,2},{5,4},{7,6},{9,8},{11,10},{13,12},{15,14},{17,16},{19,... | collective-permute-start | bytes 73736 | tf_op jit(solution)/shard_map/ppermute | solution.py:23
  73.0 4.0 %copy-start.1 = (f32[32,16,1024]{2,0,1:T(8,128)S(1)}, f32[32,16,1024]{2,0,1:T(8,128)}, u32[]{:S(2)}) copy-start(f32[32,16,1024]{2,0,1:T(8,128)} %fusion.30) | copy-start | bytes 6291460
  73.0 4.0 %copy-start.2 = (f32[16,32,1024]{2,1,0:T(8,128)S(1)}, f32[16,32,1024]{2,1,0:T(8,128)}, u32[]{:S(2)}) copy-start(f32[16,32,1024]{2,1,0:T(8,128)} %reshape.202) | copy-start | bytes 6291460
  73.0 4.0 %copy-start.4 = (f32[16,1024]{1,0:T(8,128)S(1)}, f32[16,1024]{1,0:T(8,128)}, u32[]{:S(2)}) copy-start(f32[16,1024]{1,0:T(8,128)} %get-tuple-element.32) | copy-start | bytes 196612
  73.0 4.0 %copy-start.5 = (f32[16,1024]{1,0:T(8,128)S(1)}, f32[16,1024]{1,0:T(8,128)}, u32[]{:S(2)}) copy-start(f32[16,1024]{1,0:T(8,128)} %get-tuple-element.33) | copy-start | bytes 196612
